TPU v7x, 32 devices: a whole 2x2x4 slice. The times are simulated.
32 devices in a mesh: atoms: 32 (over z, y, x, core).
Axes of the slice: x: 2, y: 2, z: 4, core: 2. Of those that a mesh axis runs over, the one named last changes fastest.
Arguments:
- features: bfloat16 [4096, 9, 128], P('atoms'), may hold values from -6 to 6
- cotangent: bfloat16 [4096, 9, 128], P('atoms'), may hold values from -6 to 6
- wigner: float32 [9, 9, 12288], P(None, None, 'atoms'), may hold values from -1 to 1, as said below
- pair_blocks: int32 [512, 2], P('atoms'), may hold values from 0 to 31, all different within a row; in each aligned block of 16 rows (0 to 15, 16 to 31, ...) at most 2 rows name the same one
- pair_rows: int32 [2, 6, 512], P(None, None, 'atoms'), may hold values from 0 to 127
- edge_ends: int32 [2, 12288], P(None, 'atoms'), may hold values from 0 to 5
- first_m0: bfloat16 [768, 512], replicated, may hold values from -0.21875 to 0.21875
- first_m1: bfloat16 [2, 512, 256], replicated, may hold values from -0.1875 to 0.1875
- first_m2: bfloat16 [2, 256, 128], replicated, may hold values from -0.25 to 0.25
- second_m0: bfloat16 [384, 384], replicated, may hold values from -0.3125 to 0.3125
- second_m1: bfloat16 [2, 256, 256], replicated, may hold values from -0.25 to 0.25
- second_m2: bfloat16 [2, 128, 128], replicated, may hold values from -0.375 to 0.375
Outputs:
- messages: bfloat16 [4096, 9, 128], P('atoms')
- grad_features: float32 [4096, 9, 128], P('atoms')
- grad_first_m0: float32 [768, 512], replicated
- grad_first_m1: float32 [2, 512, 256], replicated
- grad_first_m2: float32 [2, 256, 128], replicated
- grad_second_m0: float32 [384, 384], replicated
- grad_second_m1: float32 [2, 256, 256], replicated
- grad_second_m2: float32 [2, 128, 128], replicated
Inputs may be any that keep to these rules, and one draw needn't show every extreme that they name: `pair_blocks`: among the 16 pairs of one device no atom block is named more than 2 times; the two blocks of a pair differ. `wigner`: each edge's matrix is orthogonal and block diagonal over degrees 0, 1 and 2.
All inputs are finite; a program needn't handle non-finite values.
Results may differ from a plain program's by a relative error of at most 0.0045.
Values may be sent and summed in bfloat16 or wider, within the bound.
A program may use at most 128 MiB of HBM per device.

v0:
```python
import jax
import jax.numpy as jnp
from jax import lax
from jax.experimental import pallas as pl
from jax.experimental.pallas import tpu as pltpu
from jax.sharding import PartitionSpec as P

COEF_ORDER = (0, 2, 6, 3, 7, 1, 5, 8, 4)
DEGREES = ((0, 1), (1, 4), (4, 9))
CHUNK = 128
LANES = 128
VMEM_BYTES = 66_000_000


def degree_of(index):
    for low, high in DEGREES:
        if low <= index < high:
            return range(low, high)


def dot_nn(left, right):
    return jnp.dot(left, right, preferred_element_type=jnp.float32)


def dot_nt(left, right):
    return lax.dot_general(left, right, (((1,), (1,)), ((), ())), preferred_element_type=jnp.float32)


def dot_tn(left, right):
    return lax.dot_general(left, right, (((0,), (0,)), ((), ())), preferred_element_type=jnp.float32)


def pick_kernel(picked_ref, features_ref, cotangent_ref, out_ref):
    rows = out_ref.shape[0]
    coefs, atoms, channels = features_ref.shape
    chosen = picked_ref[...] == lax.broadcasted_iota(jnp.int32, (rows, atoms), 1)
    chosen = chosen.astype(jnp.float32).astype(jnp.bfloat16)
    for side, ref in enumerate((features_ref, cotangent_ref)):
        for j in range(coefs):
            at = (side * coefs + j) * channels
            out_ref[:, at : at + channels] = dot_nn(chosen, ref[j]).astype(jnp.bfloat16)


def owner_kernel(picked_ref, back_ref, messages_ref, grads_ref):
    rows = back_ref.shape[0]
    coefs, atoms, channels = grads_ref.shape
    chosen = picked_ref[...] == lax.broadcasted_iota(jnp.int32, (rows, atoms), 1)
    chosen = chosen.astype(jnp.float32).astype(jnp.bfloat16)
    for j in range(coefs):
        at = j * channels
        messages_ref[j] = dot_tn(chosen, back_ref[:, at : at + channels]).astype(jnp.bfloat16)
        at = (coefs + j) * channels
        grads_ref[j] = dot_tn(chosen, back_ref[:, at : at + channels])


def spread_kernel(packed_ref, *out_refs):
    at = 0
    for ref in out_refs:
        views = [ref] if len(ref.shape) == 2 else [ref.at[0], ref.at[1]]
        for view in views:
            height, width = view.shape
            for col in range(0, width, LANES):
                view[:, col : col + LANES] = packed_ref[at : at + height, :].astype(jnp.float32)
                at += height


def widen_into(ref, pair_ref):
    rows, cols = pair_ref.shape[1], pair_ref.shape[2]
    ref[:rows, :cols] = pair_ref[0]
    ref[:rows, cols:] = pair_ref[1]
    ref[rows:, :cols] = (-pair_ref[1].astype(jnp.float32)).astype(jnp.bfloat16)
    ref[rows:, cols:] = pair_ref[0]


def edge_kernel(
    flat_ref, wig_ref, pos_ref, fa0, fa1, fa2, sb0, sb1, sb2,
    slots_ref, packed_ref,
    acc, wa1, wa2, wb1, wb2, ga0, ga1, ga2, gb0, gb1, gb2,
    got, z, hid, gate_ref, act, mixed, dmix, dout, dz, contrib,
):
    C = LANES
    n_slots = flat_ref.shape[0]
    edges = wig_ref.shape[0]
    half = 9 * C
    widen_into(wa1, fa1)
    widen_into(wa2, fa2)
    widen_into(wb1, sb1)
    widen_into(wb2, sb2)
    for ref in (acc, ga0, ga1, ga2, gb0, gb1, gb2):
        ref[...] = jnp.zeros_like(ref)

    def step(index, carry):
        base = pl.multiple_of(index * CHUNK, CHUNK)
        span = pl.ds(base, CHUNK)
        slot_ids = lax.broadcasted_iota(jnp.int32, (CHUNK, n_slots), 1)

        def one_hot(which):
            hit = pos_ref[span, which : which + 1] == slot_ids
            return hit.astype(jnp.float32).astype(jnp.bfloat16)

        hot = jnp.concatenate([one_hot(0), one_hot(1)], axis=0)
        for c in range(0, 2 * half, 256):
            got[:, c : c + 256] = dot_nn(hot, flat_ref[:, c : c + 256])
        T, S = slice(0, CHUNK), slice(CHUNK, 2 * CHUNK)
        wig = wig_ref[span, :]

        def entry(row, col):
            k = row * 9 + col
            return jnp.broadcast_to(wig[:, k : k + 1], (CHUNK, C))

        for i, o in enumerate(COEF_ORDER):
            sums = [None] * 4
            for j in degree_of(o):
                w = entry(o, j)
                parts = (
                    got[T, j * C : (j + 1) * C],
                    got[S, j * C : (j + 1) * C],
                    got[T, half + j * C : half + (j + 1) * C],
                    got[S, half + j * C : half + (j + 1) * C],
                )
                sums = [w * p if s is None else s + w * p for s, p in zip(sums, parts)]
            rt, rs, ct, cs = (s.astype(jnp.bfloat16) for s in sums)
            left = slice(2 * i * C, (2 * i + 1) * C)
            right = slice((2 * i + 1) * C, (2 * i + 2) * C)
            z[T, left] = rs
            z[T, right] = rt
            z[S, left] = rt
            z[S, right] = rs
            dmix[T, i * C : (i + 1) * C] = ct
            dmix[S, i * C : (i + 1) * C] = cs

        first = dot_nn(z[:, : 6 * C], fa0[...])
        hid[:, : 3 * C] = first[:, : 3 * C]
        gate_ref[...] = jax.nn.sigmoid(first[:, 3 * C :])
        hid[:, 3 * C : 7 * C] = dot_nn(z[:, 6 * C : 14 * C], wa1[...])
        hid[:, 7 * C :] = dot_nn(z[:, 14 * C :], wa2[...])
        gate = gate_ref[...]
        h0 = hid[:, :C]
        act[:, :C] = (h0 * jax.nn.sigmoid(h0)).astype(jnp.bfloat16)
        for k in range(1, 9):
            act[:, k * C : (k + 1) * C] = (hid[:, k * C : (k + 1) * C] * gate).astype(jnp.bfloat16)
        mixed[:, : 3 * C] = dot_nn(act[:, : 3 * C], sb0[...])
        mixed[:, 3 * C : 7 * C] = dot_nn(act[:, 3 * C : 7 * C], wb1[...])
        mixed[:, 7 * C :] = dot_nn(act[:, 7 * C :], wb2[...])

        gb0[...] += dot_tn(act[:, : 3 * C], dmix[:, : 3 * C])
        gb1[...] += dot_tn(act[:, 3 * C : 7 * C], dmix[:, 3 * C : 7 * C])
        gb2[...] += dot_tn(act[:, 7 * C :], dmix[:, 7 * C :])
        dact = dz
        dact[:, : 3 * C] = dot_nt(dmix[:, : 3 * C], sb0[...])
        dact[:, 3 * C : 7 * C] = dot_nt(dmix[:, 3 * C : 7 * C], wb1[...])
        dact[:, 7 * C : 9 * C] = dot_nt(dmix[:, 7 * C :], wb2[...])
        head = jax.nn.sigmoid(h0)
        dout[:, :C] = (dact[:, :C] * head * (1.0 + h0 * (1.0 - head))).astype(jnp.bfloat16)
        grad_gate = None
        for k in range(1, 9):
            d = dact[:, k * C : (k + 1) * C]
            term = d * hid[:, k * C : (k + 1) * C]
            grad_gate = term if grad_gate is None else grad_gate + term
            at = k * C if k < 3 else (k + 1) * C
            dout[:, at : at + C] = (d * gate).astype(jnp.bfloat16)
        dout[:, 3 * C : 4 * C] = (grad_gate * gate * (1.0 - gate)).astype(jnp.bfloat16)

        ga0[...] += dot_tn(z[:, : 6 * C], dout[:, : 4 * C])
        ga1[...] += dot_tn(z[:, 6 * C : 14 * C], dout[:, 4 * C : 8 * C])
        ga2[...] += dot_tn(z[:, 14 * C :], dout[:, 8 * C :])
        dz[:, : 6 * C] = dot_nt(dout[:, : 4 * C], fa0[...])
        dz[:, 6 * C : 14 * C] = dot_nt(dout[:, 4 * C : 8 * C], wa1[...])
        dz[:, 14 * C :] = dot_nt(dout[:, 8 * C :], wa2[...])

        for j in range(9):
            sums = [None] * 4
            for i, o in enumerate(COEF_ORDER):
                if o not in degree_of(j):
                    continue
                w = entry(o, j)
                left = slice(2 * i * C, (2 * i + 1) * C)
                right = slice((2 * i + 1) * C, (2 * i + 2) * C)
                parts = (
                    mixed[T, i * C : (i + 1) * C],
                    mixed[S, i * C : (i + 1) * C],
                    dz[T, right] + dz[S, left],
                    dz[T, left] + dz[S, right],
                )
                sums = [w * p if s is None else s + w * p for s, p in zip(sums, parts)]
            for row, col, value in (
                (0, j * C, sums[0]),
                (CHUNK, j * C, sums[1]),
                (0, half + j * C, sums[2]),
                (CHUNK, half + j * C, sums[3]),
            ):
                upper = value.astype(jnp.bfloat16)
                contrib[row : row + CHUNK, col : col + C] = upper
                contrib[2 * CHUNK + row : 3 * CHUNK + row, col : col + C] = (
                    value - upper.astype(jnp.float32)
                ).astype(jnp.bfloat16)
        hot_twice = jnp.concatenate([hot, hot], axis=0)
        for c in range(0, 2 * half, 256):
            acc[:, c : c + 256] += dot_tn(hot_twice, contrib[:, c : c + 256])
        return carry

    lax.fori_loop(0, edges // CHUNK, step, 0)
    slots_ref[...] = acc[...].astype(jnp.bfloat16)

    at = 0

    def put(value):
        nonlocal at
        height = value.shape[0]
        for col in range(0, value.shape[1], C):
            packed_ref[at : at + height, :] = value[:, col : col + C].astype(jnp.bfloat16)
            at += height

    def put_pair(ref):
        rows, cols = ref.shape[0] // 2, ref.shape[1] // 2
        put(ref[:rows, :cols] + ref[rows:, cols:])
        put(ref[:rows, cols:] - ref[rows:, :cols])

    put(ga0[...])
    put_pair(ga1)
    put_pair(ga2)
    put(gb0[...])
    put_pair(gb1)
    put_pair(gb2)
    rest = packed_ref.shape[0] - at
    if rest:
        packed_ref[at:, :] = jnp.zeros((rest, C), jnp.bfloat16)


def call(kernel, out_shape, scratch=(), flops=1_000_000):
    many = isinstance(out_shape, (tuple, list))
    whole = pl.BlockSpec(memory_space=pltpu.VMEM)

    def run(*operands):
        return pl.pallas_call(
            kernel,
            out_shape=out_shape,
            in_specs=[whole] * len(operands),
            out_specs=[whole] * len(out_shape) if many else whole,
            scratch_shapes=list(scratch),
            compiler_params=pltpu.CompilerParams(vmem_limit_bytes=VMEM_BYTES),
            cost_estimate=pl.CostEstimate(flops=flops, bytes_accessed=4_000_000, transcendentals=0),
        )(*operands)

    return run


def exchange(value):
    return lax.all_to_all(value, "atoms", split_axis=0, concat_axis=0, tiled=True)


def local(features, cotangent, wigner, pair_blocks, pair_rows, edge_ends, *weights):
    peers = lax.axis_size("atoms")
    atoms, coefs, channels = features.shape
    pair_count = pair_blocks.shape[0]
    row_width = pair_rows.shape[1]
    edges = edge_ends.shape[1]
    per_pair = edges // pair_count
    slot_count = max(2, 4 * pair_count // peers)
    width = slot_count * row_width
    padded = -(-width // 16) * 16
    both = 2 * coefs * channels
    f32, bf16 = jnp.float32, jnp.bfloat16

    owners = pair_blocks.reshape(2 * pair_count)
    spots = jnp.arange(2 * pair_count, dtype=jnp.int32)
    rank = jnp.sum(
        (owners[:, None] == owners[None, :]) & (spots[:, None] > spots[None, :]), axis=1
    ).astype(jnp.int32)
    end_rows = jnp.transpose(pair_rows, (2, 0, 1)).reshape(2 * pair_count, row_width)
    place = owners * slot_count + rank
    names = jnp.arange(peers * slot_count, dtype=jnp.int32)
    request = jnp.sum(
        jnp.where((place[None, :] == names[:, None])[:, :, None], end_rows[None], 0), axis=1
    ).astype(jnp.int32)
    requested = exchange(request.reshape(peers, width))
    picked = jnp.pad(requested, ((0, 0), (0, padded - width)), constant_values=-1)
    picked = picked.reshape(peers * padded, 1)

    n_slots = peers * padded
    chosen = call(pick_kernel, jax.ShapeDtypeStruct((n_slots, both), bf16))(
        picked, jnp.transpose(features, (1, 0, 2)), jnp.transpose(cotangent, (1, 0, 2))
    )
    flat = exchange(chosen.reshape(peers, padded, both)).reshape(n_slots, both)

    end_slot = (owners * padded + rank * row_width).reshape(pair_count, 1, 2)
    ends = jnp.broadcast_to(end_slot, (pair_count, per_pair, 2)).reshape(edges, 2)
    positions = ends + jnp.transpose(edge_ends)
    wig = jnp.transpose(wigner.reshape(coefs * coefs, edges))

    total_rows = sum(w.size for w in weights) // LANES
    share = -(-total_rows // (16 * peers)) * 16
    rows = 2 * CHUNK
    V = pltpu.VMEM
    first_m0, first_m1, first_m2, second_m0, second_m1, second_m2 = weights
    wide = [(2 * w.shape[1], 2 * w.shape[2]) for w in (first_m1, first_m2, second_m1, second_m2)]
    scratch = [
        V((n_slots, both), f32),
        *[V(shape, bf16) for shape in wide],
        V(first_m0.shape, f32), V(wide[0], f32), V(wide[1], f32),
        V(second_m0.shape, f32), V(wide[2], f32), V(wide[3], f32),
        V((rows, both), f32),
        V((rows, both), bf16),
        V((rows, coefs * channels), f32),
        V((rows, channels), f32),
        V((rows, coefs * channels), bf16),
        V((rows, coefs * channels), f32),
        V((rows, coefs * channels), bf16),
        V((rows, (coefs + 1) * channels), bf16),
        V((rows, both), f32),
        V((2 * rows, both), bf16),
    ]
    slots, packed = call(
        edge_kernel,
        [
            jax.ShapeDtypeStruct((n_slots, both), bf16),
            jax.ShapeDtypeStruct((peers * share, LANES), bf16),
        ],
        scratch,
        flops=10_000_000_000,
    )(flat, wig, positions, *weights)

    grad_scale = (2.0 * edges * peers) ** (-0.5)
    parts = exchange(packed.reshape(peers, share, LANES))
    back = exchange(slots.reshape(peers, padded, both)).reshape(n_slots, both)
    mine = (jnp.sum(parts.astype(f32), axis=0) * grad_scale).astype(bf16)
    everyone = exchange(jnp.broadcast_to(mine[None], (peers, share, LANES)))
    messages, grads = call(
        owner_kernel,
        [
            jax.ShapeDtypeStruct((coefs, atoms, channels), bf16),
            jax.ShapeDtypeStruct((coefs, atoms, channels), f32),
        ],
    )(picked, back)
    outs = call(spread_kernel, [jax.ShapeDtypeStruct(w.shape, f32) for w in weights])(
        everyone.reshape(peers * share, LANES)
    )
    return (jnp.transpose(messages, (1, 0, 2)), jnp.transpose(grads, (1, 0, 2)), *outs)


def solution(mesh):
    in_specs = (
        P("atoms", None, None),
        P("atoms", None, None),
        P(None, None, "atoms"),
        P("atoms", None),
        P(None, None, "atoms"),
        P(None, "atoms"),
        P(),
        P(),
        P(),
        P(),
        P(),
        P(),
    )
    out_specs = (P("atoms", None, None), P("atoms", None, None), P(), P(), P(), P(), P(), P())
    return jax.shard_map(local, mesh=mesh, in_specs=in_specs, out_specs=out_specs, check_vma=False)
```

profile of v0, /device:TPU:0, one launch (start us, length us, event | category | flops | bytes accessed | tf_op | source)
XLA Modules:
  0.0 271.4 jit_solution(189484222997925559)
XLA Ops:
  0.6 0.8 copy.53
  1.4 0.1 reshape.94
  1.5 0.2 convert_reduce_fusion.1
  1.7 0.1 iota_compare_fusion
  1.7 0.8 copy.54
  2.5 0.1 copy.55
  2.6 0.1 select_reduce_fusion
  2.7 0.1 copy.56
  2.8 0.1 all_to_all.20
  2.9 14.3 %all_to_all.32 = s32[32,1,12]{2,1,0:T(1,128)S(1)} all-to-all(s32[32,1,12]{2,1,0:T(1,128)S(1)} %bitcast.26), channel_id=1, replica_groups=mesh['atoms'=32] {'atoms'}, dimensions={0} | all-to-all | bytes 3072 | tf_op jit(solution)/shard_map/all_to_all | solution.py:249
  17.2 0.9 reshape.104.picked_ref
  18.1 3.4 %shard_map.179 = bf16[512,2304]{1,0:T(8,128)(2,1)} custom-call(s32[512,1]{1,0:T(8,128)} %reshape.104.picked_ref, bf16[9,128,128]{2,1,0:T(8,128)(2,1)} %bitcast.23, bf16[9,128,128]{2,1,0:T(8,128)(2,1)} %bitcast.24), custom_call_target="tpu_custom_call" | custom-call | flops 1000000 | bytes 4000000 | tf_op jit(solution)/shard_map/pallas_call | solution.py:235
  21.4 0.0 copy-start.2
  21.5 0.0 copy-start.1
  21.5 0.0 copy-start.3
  21.5 3.6 %all-to-all-start.1 = ((bf16[32,16,2304]{2,1,0:T(8,128)(2,1)}), bf16[32,16,2304]{2,1,0:T(8,128)(2,1)}, u32[]{:S(2)}, u32[]{:S(2)}) async-start(bf16[32,16,2304]{2,1,0:T(8,128)(2,1)} %bitcast.20), calls=%async_computation.1 | async-start | bytes 4718592 | tf_op jit(solution)/shard_map/all_to_all | solution.py:249
  25.1 0.1 mul.45
  25.2 0.1 copy.60
  25.3 0.0 copy-done.2
  25.3 0.1 copy.61
  25.4 0.0 copy-done.1
  25.4 0.8 copy.59
  26.2 0.0 copy-done.3
  26.2 0.1 copy.62
  26.4 0.7 bitcast_add_fusion.pos_ref
  27.1 52.5 %all-to-all-done.1 = bf16[32,16,2304]{2,1,0:T(8,128)(2,1)} async-done(((bf16[32,16,2304]{2,1,0:T(8,128)(2,1)}), bf16[32,16,2304]{2,1,0:T(8,128)(2,1)}, u32[]{:S(2)}, u32[]{:S(2)}) %all-to-all-start.1) | async-done | bytes 2359328 | tf_op jit(solution)/shard_map/all_to_all | solution.py:249
  79.6 22.5 %shard_map.180 = (bf16[512,2304]{1,0:T(8,128)(2,1)}, bf16[8192,128]{1,0:T(8,128)(2,1)}) custom-call(bf16[512,2304]{1,0:T(8,128)(2,1)} %bitcast.7.flat_ref, f32[384,81]{1,0:T(8,128)} %bitcast.25, s32[384,2]{1,0:T(8,128)} %bitcast_add_fusion.pos_ref, bf16[768,512]{1,0:T(8,128)(2,1)} %fa0.1, bf16[2,512,256]{2,1,0:T(8,128)(2,1)} %fa1.1, ...), custom_call_target="tpu_custom_call" | custom-call | flops 10000000000 | bytes 4000000 | tf_op jit(solution)/shard_map/pallas_call | solution.py:235
  102.1 52.6 %all_to_all.33 = bf16[32,256,128]{2,1,0:T(8,128)(2,1)} all-to-all(bf16[32,256,128]{2,1,0:T(8,128)(2,1)} %bitcast.22), channel_id=1, replica_groups=mesh['atoms'=32] {'atoms'}, dimensions={0} | all-to-all | bytes 4194304 | tf_op jit(solution)/shard_map/all_to_all | solution.py:249
  154.7 3.7 %all-to-all-start.2 = ((bf16[32,16,2304]{2,1,0:T(8,128)(2,1)}), bf16[32,16,2304]{2,1,0:T(8,128)(2,1)S(1)}, u32[]{:S(2)}, u32[]{:S(2)}) async-start(bf16[32,16,2304]{2,1,0:T(8,128)(2,1)} %bitcast.21), calls=%async_computation.2 | async-start | bytes 4718592 | tf_op jit(solution)/shard_map/all_to_all | solution.py:249
  158.4 1.9 convert_reduce_fusion
  160.3 52.5 %all-to-all-done.2 = bf16[32,16,2304]{2,1,0:T(8,128)(2,1)S(1)} async-done(((bf16[32,16,2304]{2,1,0:T(8,128)(2,1)}), bf16[32,16,2304]{2,1,0:T(8,128)(2,1)S(1)}, u32[]{:S(2)}, u32[]{:S(2)}) %all-to-all-start.2) | async-done | bytes 2359328 | tf_op jit(solution)/shard_map/all_to_all | solution.py:249
  212.8 0.0 copy-start
  212.8 2.1 broadcast_in_dim.43
  214.9 0.0 copy-done
  214.9 4.2 %all-to-all-start.4 = ((bf16[32,256,128]{2,1,0:T(8,128)(2,1)}), bf16[32,256,128]{2,1,0:T(8,128)(2,1)}, u32[]{:S(2)}, u32[]{:S(2)}) async-start(bf16[32,256,128]{2,1,0:T(8,128)(2,1)} %broadcast_in_dim.43), calls=%async_computation.4 | async-start | bytes 4194304 | tf_op jit(solution)/shard_map/all_to_all | solution.py:249
  219.1 3.6 %shard_map.181 = (bf16[9,128,128]{2,1,0:T(8,128)(2,1)}, f32[9,128,128]{2,1,0:T(8,128)}) custom-call(s32[512,1]{1,0:T(8,128)} %reshape.104.picked_ref, bf16[512,2304]{1,0:T(8,128)(2,1)} %bitcast.19), custom_call_target="tpu_custom_call" | custom-call | flops 1000000 | bytes 4000000 | tf_op jit(solution)/shard_map/pallas_call | solution.py:235
  222.7 45.1 %all-to-all-done.4 = bf16[32,256,128]{2,1,0:T(8,128)(2,1)} async-done(((bf16[32,256,128]{2,1,0:T(8,128)(2,1)}), bf16[32,256,128]{2,1,0:T(8,128)(2,1)}, u32[]{:S(2)}, u32[]{:S(2)}) %all-to-all-start.4) | async-done | bytes 2097184 | tf_op jit(solution)/shard_map/all_to_all | solution.py:249
  267.8 3.6 %shard_map.182 = (f32[768,512]{1,0:T(8,128)}, f32[2,512,256]{2,1,0:T(8,128)}, f32[2,256,128]{2,1,0:T(8,128)}, f32[384,384]{1,0:T(8,128)}, f32[2,256,256]{2,1,0:T(8,128)}, /*index=5*/f32[2,128,128]{2,1,0:T(8,128)}) custom-call(bf16[8192,128]{1,0:T(8,128)(2,1)} %bitcast.16.packed_ref), custom_call_target="tpu_custom_call" | custom-call | flops 1000000 | bytes 4000000 | tf_op jit(solution)/shard_map/pallas_call | solution.py:235
  (5 shorter events, 0.1 us)
Async XLA Ops:
  21.4 3.8 %copy-start.2 = (s32[16,2]{0,1:T(2,128)S(1)}, s32[16,2]{0,1:T(2,128)}, u32[]{:S(2)}) copy-start(s32[16,2]{0,1:T(2,128)} %param.15) | copy-start | bytes 388
  21.5 3.9 %copy-start.1 = (f32[9,9,384]{2,1,0:T(8,128)S(1)}, f32[9,9,384]{2,1,0:T(8,128)}, u32[]{:S(2)}) copy-start(f32[9,9,384]{2,1,0:T(8,128)} %param.14) | copy-start | bytes 373252
  21.5 4.8 %copy-start.3 = (s32[2,384]{1,0:T(2,128)S(1)}, s32[2,384]{1,0:T(2,128)}, u32[]{:S(2)}) copy-start(s32[2,384]{1,0:T(2,128)} %param.17) | copy-start | bytes 9220
  21.5 58.1 %all-to-all-start.1 = ((bf16[32,16,2304]{2,1,0:T(8,128)(2,1)}), bf16[32,16,2304]{2,1,0:T(8,128)(2,1)}, u32[]{:S(2)}, u32[]{:S(2)}) async-start(bf16[32,16,2304]{2,1,0:T(8,128)(2,1)} %bitcast.20), calls=%async_computation.1 | async-start | bytes 4718592 | tf_op jit(solution)/shard_map/all_to_all | solution.py:249
  154.7 58.1 %all-to-all-start.2 = ((bf16[32,16,2304]{2,1,0:T(8,128)(2,1)}), bf16[32,16,2304]{2,1,0:T(8,128)(2,1)S(1)}, u32[]{:S(2)}, u32[]{:S(2)}) async-start(bf16[32,16,2304]{2,1,0:T(8,128)(2,1)} %bitcast.21), calls=%async_computation.2 | async-start | bytes 4718592 | tf_op jit(solution)/shard_map/all_to_all | solution.py:249
  212.8 2.1 copy-start
  214.9 53.0 %all-to-all-start.4 = ((bf16[32,256,128]{2,1,0:T(8,128)(2,1)}), bf16[32,256,128]{2,1,0:T(8,128)(2,1)}, u32[]{:S(2)}, u32[]{:S(2)}) async-start(bf16[32,256,128]{2,1,0:T(8,128)(2,1)} %broadcast_in_dim.43), calls=%async_computation.4 | async-start | bytes 4194304 | tf_op jit(solution)/shard_map/all_to_all | solution.py:249
where the time goes:
time: 272 us; the launch traced here: 271 us
  waiting for transfers between devices  150 us (55%)
  blocking collectives  66.9 us (25%)
  Pallas kernels  33.1 us (12%)
  starting transfers between devices  11.5 us (4%)
  local copies, waits for them, and re-layouts  6.05 us (2%)
  other arithmetic  2.98 us (1%)
    all_to_all x3, waiting for transfers between devices, exchange(): lax.all_to_all(value, 'atoms', split_axis=0, concat_axis=0, tiled=True)  150 us
    all_to_all x2, blocking collectives, exchange(): lax.all_to_all(value, 'atoms', split_axis=0, concat_axis=0, tiled=True)  66.9 us
    pallas_call x4, Pallas kernels, run(): pl.pallas_call(kernel, out_shape=out_shape, in_specs=[whole] * len(operan...  33.1 us
    all_to_all x3, starting transfers between devices, exchange(): lax.all_to_all(value, 'atoms', split_axis=0, concat_axis=0, tiled=True)  11.5 us
  transfers between devices with their start and end apart: 3, of which 3 were waited for; matrix products, arithmetic and copies ran while one was open for 1% of the time, Pallas kernels for 1%

commit v1 on v0

--- a/solution.py
+++ b/solution.py
@@ -247,6 +247,12 @@
 
 def exchange(value):
     return lax.all_to_all(value, "atoms", split_axis=0, concat_axis=0, tiled=True)
+
+
+def grouped(value, groups):
+    return lax.all_to_all(
+        value, "atoms", split_axis=0, concat_axis=0, tiled=True, axis_index_groups=groups
+    )
 
 
 def local(features, cotangent, wigner, pair_blocks, pair_rows, edge_ends, *weights):
@@ -321,10 +327,18 @@
     )(flat, wig, positions, *weights)
 
     grad_scale = (2.0 * edges * peers) ** (-0.5)
-    parts = exchange(packed.reshape(peers, share, LANES))
     back = exchange(slots.reshape(peers, padded, both)).reshape(n_slots, both)
+    near_count = 8 if peers % 8 == 0 else 1
+    far_count = peers // near_count
+    near = [[h * near_count + n for n in range(near_count)] for h in range(far_count)]
+    far = [[h * near_count + n for h in range(far_count)] for n in range(near_count)]
+    parts = grouped(packed.reshape(near_count, far_count * share, LANES), near)
+    block = jnp.sum(parts.astype(f32), axis=0).astype(bf16)
+    parts = grouped(block.reshape(far_count, share, LANES), far)
     mine = (jnp.sum(parts.astype(f32), axis=0) * grad_scale).astype(bf16)
-    everyone = exchange(jnp.broadcast_to(mine[None], (peers, share, LANES)))
+    block = grouped(jnp.broadcast_to(mine[None], (far_count, share, LANES)), far)
+    block = block.reshape(1, far_count * share, LANES)
+    everyone = grouped(jnp.broadcast_to(block, (near_count, far_count * share, LANES)), near)
     messages, grads = call(
         owner_kernel,
         [

time: 272 us -> 247 us (0.908)
  waiting for transfers between devices: 150 us -> 103 us
  blocking collectives: 66.9 us -> 96.3 us
  starting transfers between devices: 11.5 us -> 7.14 us
    all_to_all x0 -> x4, blocking collectives: none -> 82 us  [grouped(): lax.all_to_all(value, 'atoms', split_axis=0, concat_axis=0, tiled=True, a...]
    all_to_all x2 -> x1, blocking collectives: 66.9 us -> 14.3 us  [exchange(): lax.all_to_all(value, 'atoms', split_axis=0, concat_axis=0, tiled=True)]
    all_to_all x3 -> x2, waiting for transfers between devices: 150 us -> 103 us  [exchange(): lax.all_to_all(value, 'atoms', split_axis=0, concat_axis=0, tiled=True)]
    all_to_all x3 -> x2, starting transfers between devices: 11.5 us -> 7.14 us  [exchange(): lax.all_to_all(value, 'atoms', split_axis=0, concat_axis=0, tiled=True)]
  transfers between devices with their start and end apart: 3 -> 2, of which waited for: 3 -> 2; matrix products, arithmetic and copies ran while one was open for 1% -> 1% of each run, Pallas kernels for 1% -> 1%
where the time goes in v1:
time: 247 us; the launch traced here: 246 us
  waiting for transfers between devices  103 us (42%)
  blocking collectives  96.3 us (39%)
  Pallas kernels  33.1 us (13%)
  starting transfers between devices  7.14 us (3%)
  local copies, waits for them, and re-layouts  4.32 us (2%)
    all_to_all x2, waiting for transfers between devices, exchange(): lax.all_to_all(value, 'atoms', split_axis=0, concat_axis=0, tiled=True)  103 us
    all_to_all x4, blocking collectives, grouped(): lax.all_to_all(value, 'atoms', split_axis=0, concat_axis=0, tiled=True, a...  82 us
    pallas_call x4, Pallas kernels, run(): pl.pallas_call(kernel, out_shape=out_shape, in_specs=[whole] * len(operan...  33.1 us
    all_to_all x1, blocking collectives, exchange(): lax.all_to_all(value, 'atoms', split_axis=0, concat_axis=0, tiled=True)  14.3 us
    all_to_all x2, starting transfers between devices, exchange(): lax.all_to_all(value, 'atoms', split_axis=0, concat_axis=0, tiled=True)  7.14 us
  transfers between devices with their start and end apart: 2, of which 2 were waited for; matrix products, arithmetic and copies ran while one was open for 1% of the time, Pallas kernels for 1%

profile of v1, /device:TPU:0, one launch (start us, length us, event | category | flops | bytes accessed | tf_op | source)
XLA Modules:
  0.0 246.4 jit_solution(825537115694171493)
XLA Ops:
  0.6 0.8 copy.53
  1.4 0.1 reshape.99
  1.5 0.2 convert_reduce_fusion.1
  1.7 0.1 iota_compare_fusion
  1.7 0.8 copy.54
  2.5 0.1 copy.55
  2.6 0.1 select_reduce_fusion
  2.7 0.1 copy.56
  2.8 0.1 all_to_all.26
  2.9 14.3 %all_to_all.42 = s32[32,1,12]{2,1,0:T(1,128)S(1)} all-to-all(s32[32,1,12]{2,1,0:T(1,128)S(1)} %bitcast.29), channel_id=1, replica_groups=mesh['atoms'=32] {'atoms'}, dimensions={0} | all-to-all | bytes 3072 | tf_op jit(solution)/shard_map/all_to_all | solution.py:249
  17.2 0.9 reshape.110.picked_ref
  18.1 3.4 %shard_map.179 = bf16[512,2304]{1,0:T(8,128)(2,1)} custom-call(s32[512,1]{1,0:T(8,128)} %reshape.110.picked_ref, bf16[9,128,128]{2,1,0:T(8,128)(2,1)} %bitcast.26, bf16[9,128,128]{2,1,0:T(8,128)(2,1)} %bitcast.27), custom_call_target="tpu_custom_call" | custom-call | flops 1000000 | bytes 4000000 | tf_op jit(solution)/shard_map/pallas_call | solution.py:235
  21.5 0.0 copy-start.1
  21.5 0.0 copy-start
  21.5 0.0 copy-start.2
  21.5 3.6 %all-to-all-start.1 = ((bf16[32,16,2304]{2,1,0:T(8,128)(2,1)}), bf16[32,16,2304]{2,1,0:T(8,128)(2,1)}, u32[]{:S(2)}, u32[]{:S(2)}) async-start(bf16[32,16,2304]{2,1,0:T(8,128)(2,1)} %bitcast.21), calls=%async_computation.1 | async-start | bytes 4718592 | tf_op jit(solution)/shard_map/all_to_all | solution.py:249
  25.1 0.1 mul.45
  25.2 0.1 copy.60
  25.3 0.0 copy-done.1
  25.3 0.1 copy.61
  25.4 0.0 copy-done
  25.4 0.8 copy.59
  26.2 0.0 copy-done.2
  26.2 0.1 copy.62
  26.4 0.7 bitcast_add_fusion.pos_ref
  27.1 52.5 %all-to-all-done.1 = bf16[32,16,2304]{2,1,0:T(8,128)(2,1)} async-done(((bf16[32,16,2304]{2,1,0:T(8,128)(2,1)}), bf16[32,16,2304]{2,1,0:T(8,128)(2,1)}, u32[]{:S(2)}, u32[]{:S(2)}) %all-to-all-start.1) | async-done | bytes 2359328 | tf_op jit(solution)/shard_map/all_to_all | solution.py:249
  79.6 22.5 %shard_map.180 = (bf16[512,2304]{1,0:T(8,128)(2,1)}, bf16[8192,128]{1,0:T(8,128)(2,1)}) custom-call(bf16[512,2304]{1,0:T(8,128)(2,1)} %bitcast.7.flat_ref, f32[384,81]{1,0:T(8,128)} %bitcast.28, s32[384,2]{1,0:T(8,128)} %bitcast_add_fusion.pos_ref, bf16[768,512]{1,0:T(8,128)(2,1)} %fa0.1, bf16[2,512,256]{2,1,0:T(8,128)(2,1)} %fa1.1, ...), custom_call_target="tpu_custom_call" | custom-call | flops 10000000000 | bytes 4000000 | tf_op jit(solution)/shard_map/pallas_call | solution.py:235
  102.1 30.1 %all_to_all.43 = bf16[8,1024,128]{2,1,0:T(8,128)(2,1)S(1)} all-to-all(bf16[8,1024,128]{2,1,0:T(8,128)(2,1)} %bitcast.23), channel_id=1, replica_groups={{0,1,2,3,4,5,6,7},{8,9,10,11,12,13,14,15},{16,17,18,19,20,21,22,23},{24..., dimensions={0} | all-to-all | bytes 4194304 | tf_op jit(solution)/shard_map/all_to_all | solution.py:253
  132.2 0.4 reduce_sum.41
  132.6 11.2 %all_to_all.44 = bf16[4,256,128]{2,1,0:T(8,128)(2,1)S(1)} all-to-all(bf16[4,256,128]{2,1,0:T(8,128)(2,1)S(1)} %bitcast.24), channel_id=1, replica_groups={{0,8,16,24},{1,9,17,25},{2,10,18,26},{3,11,19,27},{4,12,20,28},{5,13,21..., dimensions={0} | all-to-all | bytes 524288 | tf_op jit(solution)/shard_map/all_to_all | solution.py:253
  143.9 11.0 %all_to_all.45 = bf16[4,256,128]{2,1,0:T(8,128)(2,1)S(1)} all-to-all(bf16[4,256,128]{2,1,0:T(8,128)(2,1)S(1)} %broadcast_in_dim.50), channel_id=1, replica_groups={{0,8,16,24},{1,9,17,25},{2,10,18,26},{3,11,19,27},{4,12,20,28},{5,13,21..., dimensions={0} | all-to-all | bytes 524288 | tf_op jit(solution)/shard_map/all_to_all | solution.py:253
  154.8 0.3 broadcast_in_dim.52
  155.1 29.7 %all_to_all.46 = bf16[8,1024,128]{2,1,0:T(8,128)(2,1)} all-to-all(bf16[8,1024,128]{2,1,0:T(8,128)(2,1)S(1)} %broadcast_in_dim.52), channel_id=1, replica_groups={{0,1,2,3,4,5,6,7},{8,9,10,11,12,13,14,15},{16,17,18,19,20,21,22,23},{24..., dimensions={0} | all-to-all | bytes 4194304 | tf_op jit(solution)/shard_map/all_to_all | solution.py:253
  184.8 3.5 %all-to-all-start.2 = ((bf16[32,16,2304]{2,1,0:T(8,128)(2,1)}), bf16[32,16,2304]{2,1,0:T(8,128)(2,1)}, u32[]{:S(2)}, u32[]{:S(2)}) async-start(bf16[32,16,2304]{2,1,0:T(8,128)(2,1)} %bitcast.11), calls=%async_computation.2 | async-start | bytes 4718592 | tf_op jit(solution)/shard_map/all_to_all | solution.py:249
  188.4 3.6 %shard_map.182 = (f32[768,512]{1,0:T(8,128)}, f32[2,512,256]{2,1,0:T(8,128)}, f32[2,256,128]{2,1,0:T(8,128)}, f32[384,384]{1,0:T(8,128)}, f32[2,256,256]{2,1,0:T(8,128)}, /*index=5*/f32[2,128,128]{2,1,0:T(8,128)}) custom-call(bf16[8192,128]{1,0:T(8,128)(2,1)} %bitcast.22), custom_call_target="tpu_custom_call" | custom-call | flops 1000000 | bytes 4000000 | tf_op jit(solution)/shard_map/pallas_call | solution.py:235
  192.0 50.9 %all-to-all-done.2 = bf16[32,16,2304]{2,1,0:T(8,128)(2,1)} async-done(((bf16[32,16,2304]{2,1,0:T(8,128)(2,1)}), bf16[32,16,2304]{2,1,0:T(8,128)(2,1)}, u32[]{:S(2)}, u32[]{:S(2)}) %all-to-all-start.2) | async-done | bytes 2359328 | tf_op jit(solution)/shard_map/all_to_all | solution.py:249
  242.9 3.6 %shard_map.181 = (bf16[9,128,128]{2,1,0:T(8,128)(2,1)}, f32[9,128,128]{2,1,0:T(8,128)}) custom-call(s32[512,1]{1,0:T(8,128)} %reshape.110.picked_ref, bf16[512,2304]{1,0:T(8,128)(2,1)} %bitcast.12.back_ref), custom_call_target="tpu_custom_call" | custom-call | flops 1000000 | bytes 4000000 | tf_op jit(solution)/shard_map/pallas_call | solution.py:235
  (7 shorter events, 0.1 us)
Async XLA Ops:
  21.5 3.8 %copy-start.1 = (s32[16,2]{0,1:T(2,128)S(1)}, s32[16,2]{0,1:T(2,128)}, u32[]{:S(2)}) copy-start(s32[16,2]{0,1:T(2,128)} %param.15) | copy-start | bytes 388
  21.5 3.9 %copy-start = (f32[9,9,384]{2,1,0:T(8,128)S(1)}, f32[9,9,384]{2,1,0:T(8,128)}, u32[]{:S(2)}) copy-start(f32[9,9,384]{2,1,0:T(8,128)} %param.14) | copy-start | bytes 373252
  21.5 4.8 %copy-start.2 = (s32[2,384]{1,0:T(2,128)S(1)}, s32[2,384]{1,0:T(2,128)}, u32[]{:S(2)}) copy-start(s32[2,384]{1,0:T(2,128)} %param.17) | copy-start | bytes 9220
  21.5 58.1 %all-to-all-start.1 = ((bf16[32,16,2304]{2,1,0:T(8,128)(2,1)}), bf16[32,16,2304]{2,1,0:T(8,128)(2,1)}, u32[]{:S(2)}, u32[]{:S(2)}) async-start(bf16[32,16,2304]{2,1,0:T(8,128)(2,1)} %bitcast.21), calls=%async_computation.1 | async-start | bytes 4718592 | tf_op jit(solution)/shard_map/all_to_all | solution.py:249
  184.8 58.0 %all-to-all-start.2 = ((bf16[32,16,2304]{2,1,0:T(8,128)(2,1)}), bf16[32,16,2304]{2,1,0:T(8,128)(2,1)}, u32[]{:S(2)}, u32[]{:S(2)}) async-start(bf16[32,16,2304]{2,1,0:T(8,128)(2,1)} %bitcast.11), calls=%async_computation.2 | async-start | bytes 4718592 | tf_op jit(solution)/shard_map/all_to_all | solution.py:249
